TPU v7x, 128 devices: a whole 4x4x4 slice. The times are simulated.
128 devices in a mesh: dp: 32 (over z, y, core), mp: 4 (over x).
Axes of the slice: x: 4, y: 4, z: 4, core: 2. Of those that a mesh axis runs over, the one named last changes fastest.
Arguments:
- features: bfloat16 [98304, 1024], P('dp'), may hold values from -6 to 6
- curvature: bfloat16 [98304, 4096], P('dp', 'mp'), may hold values from 0.099609375 to 2
- task_grad: float32 [1024, 4096], P('dp', 'mp'), may hold values from -6 to 6
Outputs:
- solution: float32 [1024, 4096], P('dp', 'mp')
- residual: float32 [1024, 4096], P('dp', 'mp')
All inputs are finite; a program needn't handle non-finite values.
Results may differ from a plain program's by a relative error of at most 0.0095.
The roundings to bfloat16 on the way count: a program that leaves them out, or rounds other values in their place, can miss the bound.
Values may be sent and summed in bfloat16 or wider, within the bound.
A program may use at most 64 MiB of HBM per device.

v0:
```python
import jax
import jax.numpy as jnp
from jax import lax
from jax.sharding import PartitionSpec as P

ITERS = 2
damp_coef = 0.5


def weigh_rows(curvature, projected):
    return (curvature * projected).astype(jnp.bfloat16)


def shards(features, curvature, task_grad):
    token_count = features.shape[0] * lax.axis_size("dp")

    def global_sums(values):
        return lax.psum(values, ("dp", "mp"))

    solution = jnp.zeros_like(task_grad)
    residual = task_grad
    direction = task_grad
    norm_now = jnp.sum(residual * residual)
    for turn in range(ITERS):
        dir_bf = direction.astype(jnp.bfloat16)
        gathered = lax.all_gather(dir_bf, "dp", axis=0, tiled=True)
        projected = jnp.dot(features, gathered, preferred_element_type=jnp.float32)
        weighted = weigh_rows(curvature, projected)
        summed = lax.psum_scatter(
            lax.dot_general(
                features, weighted, (((0,), (0,)), ((), ())), preferred_element_type=jnp.float32
            ),
            "dp",
            scatter_dimension=0,
            tiled=True,
        )
        curved = summed / token_count + damp_coef * direction
        pdot_local = jnp.sum(direction * curved)
        if turn == 0:
            norm_now, curv_dot = global_sums((norm_now, pdot_local))
        else:
            curv_dot = global_sums(pdot_local)
        step_len = norm_now / curv_dot
        solution = solution + step_len * direction
        residual = residual - step_len * curved
        if turn + 1 < ITERS:
            norm_next = global_sums(jnp.sum(residual * residual))
        if turn + 1 < ITERS:
            direction = residual + norm_next / norm_now * direction
            norm_now = norm_next
    return (solution, residual)


def solution(mesh):
    placed = (P("dp", None), P("dp", "mp"), P("dp", "mp"))
    return jax.shard_map(
        shards,
        mesh=mesh,
        in_specs=placed,
        out_specs=(P("dp", "mp"), P("dp", "mp")),
        check_vma=False,
    )
```

profile of v0, /device:TPU:1, one launch (start us, length us, event | category | flops | bytes accessed | tf_op | source)
XLA Modules:
  0.0 527.6 jit_solution(15309340547715633252)
XLA Ops:
  7.2 0.0 all-gather.3.cloned.1.call-start
  7.2 1.5 convert_element_type.17
  8.8 0.0 reduce-scatter.7.cloned.1.call-start
  8.8 49.4 %all-gather.3.cloned.1.call-done = bf16[1024,1024]{1,0:T(8,128)(2,1)} async-done(((bf16[32,1024]{1,0:T(8,128)(2,1)}), bf16[1024,1024]{1,0:T(8,128)(2,1)}) %all-gather.3.cloned.1.call-update) | async-done | bytes 2097168 | tf_op jit(solution)/shard_map/all_gather | solution.py:26
  58.2 22.5 %fusion.4 = f32[1024,1024]{0,1:T(8,128)} fusion(bf16[3072,1024]{1,0:T(8,128)(2,1)} %param.3, bf16[3072,1024]{1,0:T(8,128)(2,1)} %param.4, bf16[1024,1024]{1,0:T(8,128)(2,1)} %all-gather.3.cloned.1.call-done), kind=kOutput, calls=%fused_computation.6 | convolution fusion | flops 12894339072 | bytes 18874368 | tf_op jit(solution)/shard_map/dot_general | solution.py:30
  80.7 5.4 %copy.24 = f32[1024,1024]{1,0:T(8,128)} copy(f32[1024,1024]{0,1:T(8,128)} %fusion.4) | data formatting | bytes 8388608
  86.0 0.0 reduce-scatter.7.cloned.1.call-update
  86.1 0.0 all-gather.5.cloned.1.call-start
  86.1 79.7 %reduce-scatter.7.cloned.1.call-done = f32[32,1024]{1,0:T(8,128)} async-done(((f32[1024,1024]{1,0:T(8,128)}), f32[32,1024]{1,0:T(8,128)}) %reduce-scatter.7.cloned.1.call-update) | async-done | bytes 131088 | tf_op jit(solution)/shard_map/reduce_scatter | solution.py:29
  165.8 1.5 multiply_reduce_fusion.2
  167.4 65.9 %all-reduce = (f32[]{:T(128)}, f32[]{:T(128)}) all-reduce(f32[]{:T(128)} %get-tuple-element.7, f32[]{:T(128)} %get-tuple-element.6), channel_id=1, replica_groups=mesh['dp'=32,'mp'=4] {'dp','mp'}, use_global_device_ids=true, to_apply=%region_1.0 | all-reduce | flops 2 | bytes 16 | tf_op jit(solution)/shard_map/psum | solution.py:18
  234.7 1.5 multiply_reduce_fusion.1
  236.2 62.5 %psum.30 = f32[]{:T(128)} all-reduce(f32[]{:T(128)} %multiply_reduce_fusion.1), channel_id=1, replica_groups=mesh['dp'=32,'mp'=4] {'dp','mp'}, use_global_device_ids=true, to_apply=%region_6.0 | all-reduce | flops 1 | bytes 8 | tf_op jit(solution)/shard_map/psum | solution.py:18
  300.1 1.6 fusion.6
  301.7 0.0 all-gather.5.cloned.1.call-update
  301.7 0.0 reduce-scatter.9.cloned.1.call-start
  301.8 41.3 %all-gather.5.cloned.1.call-done = bf16[1024,1024]{1,0:T(8,128)(2,1)} async-done(((bf16[32,1024]{1,0:T(8,128)(2,1)}), bf16[1024,1024]{1,0:T(8,128)(2,1)}) %all-gather.5.cloned.1.call-update) | async-done | bytes 2097168 | tf_op jit(solution)/shard_map/all_gather | solution.py:26
  343.1 22.3 %fusion.5 = f32[1024,1024]{0,1:T(8,128)} fusion(bf16[3072,1024]{1,0:T(8,128)(2,1)} %param.3, bf16[3072,1024]{1,0:T(8,128)(2,1)} %param.4, bf16[1024,1024]{1,0:T(8,128)(2,1)} %all-gather.5.cloned.1.call-done), kind=kOutput, calls=%fused_computation.7 | convolution fusion | flops 12894339072 | bytes 18874368 | tf_op jit(solution)/shard_map/dot_general | solution.py:30
  365.4 5.4 %copy.26 = f32[1024,1024]{1,0:T(8,128)} copy(f32[1024,1024]{0,1:T(8,128)} %fusion.5) | data formatting | bytes 8388608
  370.7 0.0 reduce-scatter.9.cloned.1.call-update
  370.8 79.8 %reduce-scatter.9.cloned.1.call-done = f32[32,1024]{1,0:T(8,128)} async-done(((f32[1024,1024]{1,0:T(8,128)}), f32[32,1024]{1,0:T(8,128)}) %reduce-scatter.9.cloned.1.call-update) | async-done | bytes 131088 | tf_op jit(solution)/shard_map/reduce_scatter | solution.py:29
  450.5 1.6 multiply_reduce_fusion
  452.1 65.9 %psum.31 = f32[]{:T(128)} all-reduce(f32[]{:T(128)} %multiply_reduce_fusion), channel_id=1, replica_groups=mesh['dp'=32,'mp'=4] {'dp','mp'}, use_global_device_ids=true, to_apply=%region_9.0 | all-reduce | flops 1 | bytes 8 | tf_op jit(solution)/shard_map/psum | solution.py:18
  519.4 1.7 multiply_subtract_fusion
  (5 shorter events, 0.0 us)
Async XLA Ops:
  7.2 51.0 %all-gather.3.cloned.1.call-start = ((), (), s32[]{:S(2)}) async-start(), calls=%async_computation.2 | async-start | bytes 2162688 | tf_op jit(solution)/shard_map/all_gather | solution.py:26
  8.8 157.1 %reduce-scatter.7.cloned.1.call-start = ((), (), s32[]{:S(2)}) async-start(), calls=%async_computation.4 | async-start | bytes 4325376 | tf_op jit(solution)/shard_map/reduce_scatter | solution.py:29
  80.7 85.2 %copy-start = (f32[32,1024]{1,0:T(8,128)S(1)}, f32[32,1024]{1,0:T(8,128)}, u32[]{:S(2)}) copy-start(f32[32,1024]{1,0:T(8,128)} %param.5) | copy-start | bytes 393220
  86.1 257.0 %all-gather.5.cloned.1.call-start = ((), (), s32[]{:S(2)}) async-start(), calls=%async_computation.3 | async-start | bytes 2162688 | tf_op jit(solution)/shard_map/all_gather | solution.py:26
  301.7 148.8 %reduce-scatter.9.cloned.1.call-start = ((), (), s32[]{:S(2)}) async-start(), calls=%async_computation.5 | async-start | bytes 4325376 | tf_op jit(solution)/shard_map/reduce_scatter | solution.py:29
  365.3 85.2 %copy-start.1 = (f32[32,1024]{1,0:T(8,128)S(1)}, f32[32,1024]{1,0:T(8,128)}, u32[]{:S(2)}) copy-start(f32[32,1024]{1,0:T(8,128)} %reduce-scatter.7.cloned.1.call-done) | copy-start | bytes 393220
Sparse Core Ops, SparseCore 0:
  10.8 47.3 all-gather.2
  86.2 79.5 reduce-scatter.6
  301.8 41.2 all-gather.4
  370.9 79.6 reduce-scatter.8
where the time goes:
time: 528 us
  waiting for transfers between devices  250 us (47%)
  blocking collectives  194 us (37%)
  matrix products  44.8 us (8%)
  between operations  17.8 us (3%)
  local copies, waits for them, and re-layouts  10.8 us (2%)
  other arithmetic  9.45 us (2%)
    psum x3, blocking collectives, global_sums(): return lax.psum(values, ('dp', 'mp'))  194 us
    reduce_scatter x2, waiting for transfers between devices, shards(): lax.psum_scatter(lax.dot_general(features, weighted, (((0,), (0,)), ((),...  160 us
    all_gather x2, waiting for transfers between devices, shards(): gathered = lax.all_gather(dir_bf, 'dp', axis=0, tiled=True)  90.7 us
    dot_general x2, matrix products, shards(): lax.dot_general(features, weighted, (((0,), (0,)), ((), ())), preferred_e...  44.8 us
    unnamed x6, local copies, waits for them, and re-layouts  10.8 us
  transfers between devices with their start and end apart: 4, of which 4 were waited for; matrix products, arithmetic and copies ran while one was open for 0% of the time, Pallas kernels for 0%

commit v1 on v0

--- a/solution.py
+++ b/solution.py
@@ -5,6 +5,12 @@
 
 ITERS = 2
 damp_coef = 0.5
+
+
+def words_name(local_array, which_axis, chip_axis):
+    for no in (which_axis, chip_axis):
+        local_array = lax.psum(local_array, no)
+    return local_array
 
 
 def weigh_rows(curvature, projected):
@@ -15,7 +21,7 @@
     token_count = features.shape[0] * lax.axis_size("dp")
 
     def global_sums(values):
-        return lax.psum(values, ("dp", "mp"))
+        return words_name(values, "dp", "mp")
 
     solution = jnp.zeros_like(task_grad)
     residual = task_grad

time: 528 us -> 556 us (1.053)
  blocking collectives: 194 us -> 220 us
    psum x3 -> x6, blocking collectives: 194 us -> 220 us  [words_name(): local_array = lax.psum(local_array, no)]
where the time goes in v1:
time: 556 us; the launch traced here: 553 us
  waiting for transfers between devices  250 us (45%)
  blocking collectives  220 us (40%)
  matrix products  44.6 us (8%)
  between operations  17.8 us (3%)
  local copies, waits for them, and re-layouts  10.8 us (2%)
  other arithmetic  9.45 us (2%)
    psum x6, blocking collectives, words_name(): local_array = lax.psum(local_array, no)  220 us
    reduce_scatter x2, waiting for transfers between devices, shards(): lax.psum_scatter(lax.dot_general(features, weighted, (((0,), (0,)), ((),...  159 us
    all_gather x2, waiting for transfers between devices, shards(): gathered = lax.all_gather(dir_bf, 'dp', axis=0, tiled=True)  90.4 us
    dot_general x2, matrix products, shards(): lax.dot_general(features, weighted, (((0,), (0,)), ((), ())), preferred_e...  44.6 us
  transfers between devices with their start and end apart: 4, of which 4 were waited for; matrix products, arithmetic and copies ran while one was open for 0% of the time, Pallas kernels for 0%

profile of v1, /device:TPU:1, one launch (start us, length us, event | category | flops | bytes accessed | tf_op | source)
XLA Modules:
  0.0 553.3 jit_solution(665560802573850543)
XLA Ops:
  7.2 0.0 all-gather.3.cloned.1.call-start
  7.2 1.5 convert_element_type.17
  8.8 0.0 reduce-scatter.7.cloned.1.call-start
  8.8 49.4 %all-gather.3.cloned.1.call-done = bf16[1024,1024]{1,0:T(8,128)(2,1)} async-done(((bf16[32,1024]{1,0:T(8,128)(2,1)}), bf16[1024,1024]{1,0:T(8,128)(2,1)}) %all-gather.3.cloned.1.call-update) | async-done | bytes 2097168 | tf_op jit(solution)/shard_map/all_gather | solution.py:32
  58.2 22.3 %fusion.4 = f32[1024,1024]{0,1:T(8,128)} fusion(bf16[3072,1024]{1,0:T(8,128)(2,1)} %param.3, bf16[3072,1024]{1,0:T(8,128)(2,1)} %param.4, bf16[1024,1024]{1,0:T(8,128)(2,1)} %all-gather.3.cloned.1.call-done), kind=kOutput, calls=%fused_computation.6 | convolution fusion | flops 12894339072 | bytes 18874368 | tf_op jit(solution)/shard_map/dot_general | solution.py:36
  80.5 5.4 copy.24
  85.9 0.0 all-gather.5.cloned.1.call-start
  85.9 79.7 %reduce-scatter.7.cloned.1.call-done = f32[32,1024]{1,0:T(8,128)} async-done(((f32[1024,1024]{1,0:T(8,128)}), f32[32,1024]{1,0:T(8,128)}) %reduce-scatter.7.cloned.1.call-update) | async-done | bytes 131088 | tf_op jit(solution)/shard_map/reduce_scatter | solution.py:35
  165.6 1.5 multiply_reduce_fusion.2
  167.2 65.0 %all-reduce = (f32[]{:T(128)}, f32[]{:T(128)}) all-reduce(f32[]{:T(128)} %get-tuple-element.7, f32[]{:T(128)} %get-tuple-element.6), channel_id=1, replica_groups=mesh['dp'=32,'mp'=4] {'dp'}, use_global_device_ids=true, to_apply=%region_1.0 | all-reduce | flops 2 | bytes 16 | tf_op jit(solution)/shard_map/psum | solution.py:12
  232.2 9.0 %all-reduce.1 = (f32[]{:T(128)}, f32[]{:T(128)}) all-reduce(f32[]{:T(128)} %get-tuple-element.8, f32[]{:T(128)} %get-tuple-element.9), channel_id=1, replica_groups=mesh['dp'=32,'mp'=4] {'mp'}, use_global_device_ids=true, to_apply=%region_2.0 | all-reduce | flops 2 | bytes 16 | tf_op jit(solution)/shard_map/psum | solution.py:12
  242.6 1.5 multiply_reduce_fusion.1
  244.1 65.7 %psum.60 = f32[]{:T(128)} all-reduce(f32[]{:T(128)} %multiply_reduce_fusion.1), channel_id=1, replica_groups=mesh['dp'=32,'mp'=4] {'dp'}, use_global_device_ids=true, to_apply=%region_8.0 | all-reduce | flops 1 | bytes 8 | tf_op jit(solution)/shard_map/psum | solution.py:12
  309.8 6.7 %psum.61 = f32[]{:T(128)} all-reduce(f32[]{:T(128)} %psum.60), channel_id=1, replica_groups=mesh['dp'=32,'mp'=4] {'mp'}, use_global_device_ids=true, to_apply=%region_9.0 | all-reduce | flops 1 | bytes 8 | tf_op jit(solution)/shard_map/psum | solution.py:12
  317.8 1.6 fusion.6
  319.4 0.2 reduce-scatter.9.cloned.1.call-start
  319.7 41.0 %all-gather.5.cloned.1.call-done = bf16[1024,1024]{1,0:T(8,128)(2,1)} async-done(((bf16[32,1024]{1,0:T(8,128)(2,1)}), bf16[1024,1024]{1,0:T(8,128)(2,1)}) %all-gather.5.cloned.1.call-update) | async-done | bytes 2097168 | tf_op jit(solution)/shard_map/all_gather | solution.py:32
  360.7 22.3 %fusion.5 = f32[1024,1024]{0,1:T(8,128)} fusion(bf16[3072,1024]{1,0:T(8,128)(2,1)} %param.3, bf16[3072,1024]{1,0:T(8,128)(2,1)} %param.4, bf16[1024,1024]{1,0:T(8,128)(2,1)} %all-gather.5.cloned.1.call-done), kind=kOutput, calls=%fused_computation.7 | convolution fusion | flops 12894339072 | bytes 18874368 | tf_op jit(solution)/shard_map/dot_general | solution.py:36
  383.0 5.4 copy.26
  388.4 79.8 %reduce-scatter.9.cloned.1.call-done = f32[32,1024]{1,0:T(8,128)} async-done(((f32[1024,1024]{1,0:T(8,128)}), f32[32,1024]{1,0:T(8,128)}) %reduce-scatter.9.cloned.1.call-update) | async-done | bytes 131088 | tf_op jit(solution)/shard_map/reduce_scatter | solution.py:35
  468.2 1.6 multiply_reduce_fusion
  469.7 65.0 %psum.62 = f32[]{:T(128)} all-reduce(f32[]{:T(128)} %multiply_reduce_fusion), channel_id=1, replica_groups=mesh['dp'=32,'mp'=4] {'dp'}, use_global_device_ids=true, to_apply=%region_12.0 | all-reduce | flops 1 | bytes 8 | tf_op jit(solution)/shard_map/psum | solution.py:12
  534.8 9.0 %psum.63 = f32[]{:T(128)} all-reduce(f32[]{:T(128)} %psum.62), channel_id=1, replica_groups=mesh['dp'=32,'mp'=4] {'mp'}, use_global_device_ids=true, to_apply=%region_13.0 | all-reduce | flops 1 | bytes 8 | tf_op jit(solution)/shard_map/psum | solution.py:12
  545.1 1.7 multiply_subtract_fusion
  (8 shorter events, 0.1 us)
Async XLA Ops:
  7.2 51.0 %all-gather.3.cloned.1.call-start = ((), (), s32[]{:S(2)}) async-start(), calls=%async_computation.2 | async-start | bytes 2162688 | tf_op jit(solution)/shard_map/all_gather | solution.py:32
  8.8 156.8 %reduce-scatter.7.cloned.1.call-start = ((), (), s32[]{:S(2)}) async-start(), calls=%async_computation.4 | async-start | bytes 4325376 | tf_op jit(solution)/shard_map/reduce_scatter | solution.py:35
  80.5 85.2 %copy-start = (f32[32,1024]{1,0:T(8,128)S(1)}, f32[32,1024]{1,0:T(8,128)}, u32[]{:S(2)}) copy-start(f32[32,1024]{1,0:T(8,128)} %param.5) | copy-start | bytes 393220
  85.9 274.9 %all-gather.5.cloned.1.call-start = ((), (), s32[]{:S(2)}) async-start(), calls=%async_computation.3 | async-start | bytes 2162688 | tf_op jit(solution)/shard_map/all_gather | solution.py:32
  319.4 148.7 %reduce-scatter.9.cloned.1.call-start = ((), (), s32[]{:S(2)}) async-start(), calls=%async_computation.5 | async-start | bytes 4325376 | tf_op jit(solution)/shard_map/reduce_scatter | solution.py:35
  383.0 85.2 %copy-start.1 = (f32[32,1024]{1,0:T(8,128)S(1)}, f32[32,1024]{1,0:T(8,128)}, u32[]{:S(2)}) copy-start(f32[32,1024]{1,0:T(8,128)} %reduce-scatter.7.cloned.1.call-done) | copy-start | bytes 393220
Sparse Core Ops, SparseCore 0:
  10.8 47.3 all-gather.2
  86.0 79.5 reduce-scatter.6
  319.6 41.1 all-gather.4
  388.5 79.5 reduce-scatter.8

commit v2 on v0

--- a/solution.py
+++ b/solution.py
@@ -23,7 +23,9 @@
     norm_now = jnp.sum(residual * residual)
     for turn in range(ITERS):
         dir_bf = direction.astype(jnp.bfloat16)
-        gathered = lax.all_gather(dir_bf, "dp", axis=0, tiled=True)
+        gathered = jnp.concatenate(
+            lax.all_to_all(jnp.stack(lax.axis_size("dp") * [dir_bf]), "dp", 0, 0), axis=0
+        )
         projected = jnp.dot(features, gathered, preferred_element_type=jnp.float32)
         weighted = weigh_rows(curvature, projected)
         summed = lax.psum_scatter(

time: 528 us -> 503 us (0.953)
  waiting for transfers between devices: 250 us -> 155 us
  blocking collectives: 194 us -> 265 us
    all_gather x2 -> x0, waiting for transfers between devices: 90.7 us -> none  [shards(): gathered = lax.all_gather(dir_bf, 'dp', axis=0, tiled=True)]
    all_to_all x0 -> x2, blocking collectives: none -> 71.1 us  [shards(): lax.all_to_all(jnp.stack(lax.axis_size('dp') * [dir_bf]), 'dp', 0, 0)]
  transfers between devices with their start and end apart: 4 -> 2, of which waited for: 4 -> 2; matrix products, arithmetic and copies ran while one was open for 0% -> 0% of each run, Pallas kernels for 0% -> 0%
where the time goes in v2:
time: 503 us; the launch traced here: 502 us
  blocking collectives  265 us (53%)
  waiting for transfers between devices  155 us (31%)
  matrix products  43.6 us (9%)
  between operations  18.1 us (4%)
  local copies, waits for them, and re-layouts  11.3 us (2%)
  other arithmetic  8.19 us (2%)
    psum x3, blocking collectives, global_sums(): return lax.psum(values, ('dp', 'mp'))  194 us
    reduce_scatter x2, waiting for transfers between devices, shards(): lax.psum_scatter(lax.dot_general(features, weighted, (((0,), (0,)), ((),...  155 us
    all_to_all x2, blocking collectives, shards(): lax.all_to_all(jnp.stack(lax.axis_size('dp') * [dir_bf]), 'dp', 0, 0)  71.1 us
    dot_general x2, matrix products, shards(): lax.dot_general(features, weighted, (((0,), (0,)), ((), ())), preferred_e...  43.6 us
    unnamed x6, local copies, waits for them, and re-layouts  10.8 us
  transfers between devices with their start and end apart: 2, of which 2 were waited for; matrix products, arithmetic and copies ran while one was open for 0% of the time, Pallas kernels for 0%

profile of v2, /device:TPU:1, one launch (start us, length us, event | category | flops | bytes accessed | tf_op | source)
XLA Modules:
  0.0 501.8 jit_solution(7328540066211113691)
XLA Ops:
  7.2 0.0 reduce-scatter.7.cloned.1.call-start
  7.2 0.9 convert_element_type.17
  8.1 0.2 stack.4
  8.4 37.7 %all_to_all.10 = bf16[32,32,1024]{2,1,0:T(8,128)(2,1)S(1)} all-to-all(bf16[32,32,1024]{2,1,0:T(8,128)(2,1)S(1)} %stack.4), channel_id=1, replica_groups=mesh['dp'=32,'mp'=4] {'dp'}, dimensions={0} | all-to-all | bytes 4194304 | tf_op jit(solution)/shard_map/all_to_all | solution.py:27
  46.1 21.9 %fusion.4 = f32[1024,1024]{0,1:T(8,128)} fusion(bf16[3072,1024]{1,0:T(8,128)(2,1)} %param.3, bf16[3072,1024]{1,0:T(8,128)(2,1)} %param.4, bf16[1024,1024]{1,0:T(8,128)(2,1)S(1)} %bitcast.20), kind=kOutput, calls=%fused_computation.6 | convolution fusion | flops 12894339072 | bytes 18874368 | tf_op jit(solution)/shard_map/dot_general | solution.py:32
  68.0 5.4 %copy.25 = f32[1024,1024]{1,0:T(8,128)} copy(f32[1024,1024]{0,1:T(8,128)} %fusion.4) | data formatting | bytes 8388608
  73.4 0.0 reduce-scatter.7.cloned.1.call-update
  73.4 0.0 reduce-scatter.9.cloned.1.call-start
  73.4 78.5 %reduce-scatter.7.cloned.1.call-done = f32[32,1024]{1,0:T(8,128)} async-done(((f32[1024,1024]{1,0:T(8,128)}), f32[32,1024]{1,0:T(8,128)}) %reduce-scatter.7.cloned.1.call-update) | async-done | bytes 131088 | tf_op jit(solution)/shard_map/reduce_scatter | solution.py:31
  151.9 0.0 copy-done
  151.9 1.5 multiply_reduce_fusion.2
  153.4 65.9 %all-reduce = (f32[]{:T(128)}, f32[]{:T(128)}) all-reduce(f32[]{:T(128)} %get-tuple-element.7, f32[]{:T(128)} %get-tuple-element.6), channel_id=1, replica_groups=mesh['dp'=32,'mp'=4] {'dp','mp'}, use_global_device_ids=true, to_apply=%region_1.0 | all-reduce | flops 2 | bytes 16 | tf_op jit(solution)/shard_map/psum | solution.py:18
  220.7 1.5 multiply_reduce_fusion.1
  222.2 62.5 %psum.30 = f32[]{:T(128)} all-reduce(f32[]{:T(128)} %multiply_reduce_fusion.1), channel_id=1, replica_groups=mesh['dp'=32,'mp'=4] {'dp','mp'}, use_global_device_ids=true, to_apply=%region_6.0 | all-reduce | flops 1 | bytes 8 | tf_op jit(solution)/shard_map/psum | solution.py:18
  286.1 0.9 fusion.6
  287.0 0.2 stack.5
  287.3 33.4 %all_to_all.11 = bf16[32,32,1024]{2,1,0:T(8,128)(2,1)S(1)} all-to-all(bf16[32,32,1024]{2,1,0:T(8,128)(2,1)S(1)} %stack.5), channel_id=1, replica_groups=mesh['dp'=32,'mp'=4] {'dp'}, dimensions={0} | all-to-all | bytes 4194304 | tf_op jit(solution)/shard_map/all_to_all | solution.py:27
  320.7 21.7 %fusion.5 = f32[1024,1024]{0,1:T(8,128)} fusion(bf16[3072,1024]{1,0:T(8,128)(2,1)} %param.3, bf16[3072,1024]{1,0:T(8,128)(2,1)} %param.4, bf16[1024,1024]{1,0:T(8,128)(2,1)S(1)} %bitcast.21), kind=kOutput, calls=%fused_computation.7 | convolution fusion | flops 12894339072 | bytes 18874368 | tf_op jit(solution)/shard_map/dot_general | solution.py:32
  342.5 5.4 %copy.27 = f32[1024,1024]{1,0:T(8,128)} copy(f32[1024,1024]{0,1:T(8,128)} %fusion.5) | data formatting | bytes 8388608
  347.8 0.0 reduce-scatter.9.cloned.1.call-update
  347.9 76.6 %reduce-scatter.9.cloned.1.call-done = f32[32,1024]{1,0:T(8,128)} async-done(((f32[1024,1024]{1,0:T(8,128)}), f32[32,1024]{1,0:T(8,128)}) %reduce-scatter.9.cloned.1.call-update) | async-done | bytes 131088 | tf_op jit(solution)/shard_map/reduce_scatter | solution.py:31
  424.5 1.6 multiply_reduce_fusion
  426.1 65.9 %psum.31 = f32[]{:T(128)} all-reduce(f32[]{:T(128)} %multiply_reduce_fusion), channel_id=1, replica_groups=mesh['dp'=32,'mp'=4] {'dp','mp'}, use_global_device_ids=true, to_apply=%region_9.0 | all-reduce | flops 1 | bytes 8 | tf_op jit(solution)/shard_map/psum | solution.py:18
  493.3 1.7 multiply_subtract_fusion
  (3 shorter events, 0.0 us)
Async XLA Ops:
  7.2 144.7 %reduce-scatter.7.cloned.1.call-start = ((), (), s32[]{:S(2)}) async-start(), calls=%async_computation.4 | async-start | bytes 4325376 | tf_op jit(solution)/shard_map/reduce_scatter | solution.py:31
  68.0 83.9 %copy-start = (f32[32,1024]{1,0:T(8,128)S(1)}, f32[32,1024]{1,0:T(8,128)}, u32[]{:S(2)}) copy-start(f32[32,1024]{1,0:T(8,128)} %param.5) | copy-start | bytes 393220
  73.4 351.1 %reduce-scatter.9.cloned.1.call-start = ((), (), s32[]{:S(2)}) async-start(), calls=%async_computation.5 | async-start | bytes 4325376 | tf_op jit(solution)/shard_map/reduce_scatter | solution.py:31
  342.4 82.0 %copy-start.1 = (f32[32,1024]{1,0:T(8,128)S(1)}, f32[32,1024]{1,0:T(8,128)}, u32[]{:S(2)}) copy-start(f32[32,1024]{1,0:T(8,128)} %reduce-scatter.7.cloned.1.call-done) | copy-start | bytes 393220
Sparse Core Ops, SparseCore 0:
  73.5 78.3 reduce-scatter.6
  348.0 76.4 reduce-scatter.8
